TPU v7x, 32 devices: a whole 2x2x4 slice. The times are simulated.
32 devices in a mesh: dp: 4 (over x, core), gx: 2 (over y), gy: 4 (over z).
Axes of the slice: x: 2, y: 2, z: 4, core: 2. Of those that a mesh axis runs over, the one named last changes fastest.
Arguments:
- inputs: bfloat16 [4096, 960], P(('dp', 'gx', 'gy')), may hold values from -6 to 6
- segments: int32 [4096], P('dp'), may hold values from 0 to 15, never falling along the last dimension, each value on 1 to 512 neighbouring positions
- attn_gain: float32 [960], replicated, may hold values from 0.5 to 1.5
- query_weight: bfloat16 [960, 960], P('gx', 'gy'), may hold values from -1.6 to 1.6
- key_weight: bfloat16 [960, 320], P('gx', 'gy'), may hold values from -1.6 to 1.6
- value_weight: bfloat16 [960, 320], P('gx', 'gy'), may hold values from -0.1875 to 0.1875
- output_weight: bfloat16 [960, 960], P('gx', 'gy'), may hold values from -0.75 to 0.75
- mlp_gain: float32 [960], replicated, may hold values from 0.5 to 1.5
- gate_weight: bfloat16 [960, 2560], P('gx', 'gy'), may hold values from -0.1875 to 0.1875
- up_weight: bfloat16 [960, 2560], P('gx', 'gy'), may hold values from -0.1875 to 0.1875
- down_weight: bfloat16 [2560, 960], P('gx', 'gy'), may hold values from -0.125 to 0.125
- cotangent: bfloat16 [4096, 960], P(('dp', 'gx', 'gy')), may hold values from -6 to 6
Outputs:
- layer_out: bfloat16 [4096, 960], P(('dp', 'gx', 'gy'))
- input_grad: bfloat16 [4096, 960], P(('dp', 'gx', 'gy'))
- query_grad: float32 [960, 960], P('gx', 'gy')
- key_grad: float32 [960, 320], P('gx', 'gy')
- value_grad: float32 [960, 320], P('gx', 'gy')
- output_grad: float32 [960, 960], P('gx', 'gy')
- gate_grad: float32 [960, 2560], P('gx', 'gy')
- up_grad: float32 [960, 2560], P('gx', 'gy')
- down_grad: float32 [2560, 960], P('gx', 'gy')
- attgain_grad: float32 [960], replicated
- mlpgain_grad: float32 [960], replicated
Inputs may be any that keep to these rules, and one draw needn't show every extreme that they name: `segments`: segment numbers never fall along the tokens; a document may run on past the end of a sequence.
All inputs are finite; a program needn't handle non-finite values.
Results may differ from a plain program's by a relative error of at most 0.04.
Values may be sent and summed in bfloat16 or wider, within the bound.
A program may use at most 128 MiB of HBM per device.

v0:
```python
import jax
import jax.numpy as jnp
from jax import lax
from jax.sharding import PartitionSpec as P

QUERY_HEADS = 15
KEY_VALUE_HEADS = 5
HEAD_WIDTH = 64
SEQUENCE_LENGTH = 1024
THETA = 100000.0
EPSILON = 1e-05
MASKED = -1e30


def rope_angles(positions):
    half_dim = HEAD_WIDTH // 2
    inverse = THETA ** (-(jnp.arange(half_dim, dtype=jnp.float32) * 2.0 / HEAD_WIDTH))
    angles = positions[:, None] * inverse[None, :]
    return (jnp.cos(angles)[:, None, :], jnp.sin(angles)[:, None, :])


def rotate(values, cos_table, sin_table):
    item_count = values.shape[0]
    shaped = values.reshape(item_count, -1, HEAD_WIDTH)
    half_dim = HEAD_WIDTH // 2
    front_part = shaped[:, :, :half_dim]
    back_part = shaped[:, :, half_dim:]
    turned = jnp.concatenate(
        [
            front_part * cos_table - back_part * sin_table,
            back_part * cos_table + front_part * sin_table,
        ],
        axis=2,
    )
    return turned.reshape(item_count, -1)


def unrotate(values, cos_table, sin_table):
    item_count = values.shape[0]
    shaped = values.reshape(item_count, -1, HEAD_WIDTH)
    half_dim = HEAD_WIDTH // 2
    front_part = shaped[:, :, :half_dim]
    back_part = shaped[:, :, half_dim:]
    turned = jnp.concatenate(
        [
            front_part * cos_table + back_part * sin_table,
            back_part * cos_table - front_part * sin_table,
        ],
        axis=2,
    )
    return turned.reshape(item_count, -1)


def normalize(values, gain):
    rms_rows = lax.rsqrt(jnp.mean(values * values, axis=1, keepdims=True) + EPSILON)
    unit_rows = values * rms_rows
    return (rms_rows, unit_rows, (unit_rows * gain).astype(jnp.bfloat16))


def normalize_back(dnormed, gain, rms_rows, unit_rows):
    scaled = dnormed * gain
    dvalues = rms_rows * (scaled - unit_rows * jnp.mean(scaled * unit_rows, axis=1, keepdims=True))
    return (dvalues, jnp.sum(dnormed * unit_rows, axis=0))


def weight_product(left, right):
    return lax.dot_general(
        left, right, (((0,), (0,)), ((), ())), preferred_element_type=jnp.float32
    )


def back_product(left, right):
    return lax.dot_general(
        left, right, (((1,), (1,)), ((), ())), preferred_element_type=jnp.float32
    )


def gather_blocks(block):
    return lax.all_gather(block, ("gx", "gy"), axis=0, tiled=False)


def whole_weight(blocks):
    fanin = lax.axis_size("gx")
    fanout = lax.axis_size("gy")
    rows, columns = blocks.shape[1:]
    shaped = blocks.reshape(fanin, fanout, rows, columns).transpose(0, 2, 1, 3)
    return shaped.reshape(fanin * rows, fanout * columns)


def cut_blocks(grad):
    fanin = lax.axis_size("gx")
    fanout = lax.axis_size("gy")
    rows, columns = (grad.shape[0] // fanin, grad.shape[1] // fanout)
    shaped = grad.astype(jnp.bfloat16).reshape(fanin, rows, fanout, columns).transpose(0, 2, 1, 3)
    return shaped.reshape(fanin * fanout, rows, columns)


def scatter_blocks(blocks):
    return lax.psum_scatter(blocks, ("gx", "gy"), scatter_dimension=0, tiled=False)


def hidden_slice(weight, groups):
    rows, columns = weight.shape
    share = rows // groups // lax.axis_size("dp")
    shaped = weight.reshape(groups, lax.axis_size("dp"), share, columns)
    picked = lax.dynamic_slice_in_dim(shaped, lax.axis_index("dp"), 1, 1)
    return picked.reshape(groups * share, columns)


def head_views(rotated_query, key_sequence, value_sequence):
    query_groups = QUERY_HEADS // KEY_VALUE_HEADS
    query_head_split = rotated_query.reshape(
        rotated_query.shape[0], KEY_VALUE_HEADS, query_groups, HEAD_WIDTH
    )
    key_head_split = key_sequence.reshape(key_sequence.shape[0], KEY_VALUE_HEADS, HEAD_WIDTH)
    value_head_split = value_sequence.reshape(value_sequence.shape[0], KEY_VALUE_HEADS, HEAD_WIDTH)
    return (query_head_split, key_head_split, value_head_split)


def masked_scores(query_head_split, key_head_split, allowed):
    scores = jnp.einsum(
        "tkgd,ukd->kgtu", query_head_split, key_head_split, preferred_element_type=jnp.float32
    ) * HEAD_WIDTH ** (-0.5)
    return jnp.where(allowed, scores, MASKED)


def attend(rotated_query, key_sequence, value_sequence, allowed):
    query_head_split, key_head_split, value_head_split = head_views(
        rotated_query, key_sequence, value_sequence
    )
    scores = masked_scores(query_head_split, key_head_split, allowed)
    highest = jnp.max(scores, axis=3, keepdims=True)
    logsum = highest + jnp.log(jnp.sum(jnp.exp(scores - highest), axis=3, keepdims=True))
    probs = jnp.exp(scores - logsum).astype(jnp.bfloat16)
    attention_mixture = jnp.einsum(
        "kgtu,ukd->tkgd", probs, value_head_split, preferred_element_type=jnp.float32
    )
    return (attention_mixture.reshape(rotated_query.shape[0], -1).astype(jnp.bfloat16), logsum)


def attend_back(
    rotated_query,
    key_sequence,
    value_sequence,
    allowed,
    logsum,
    attention_mixture,
    mixture_gradient,
):
    query_head_split, key_head_split, value_head_split = head_views(
        rotated_query, key_sequence, value_sequence
    )
    count_of_rows = rotated_query.shape[0]
    query_groups = QUERY_HEADS // KEY_VALUE_HEADS
    soft_weights = jnp.exp(masked_scores(query_head_split, key_head_split, allowed) - logsum)
    probs = soft_weights.astype(jnp.bfloat16)
    mixture_head_gradient = mixture_gradient.reshape(
        count_of_rows, KEY_VALUE_HEADS, query_groups, HEAD_WIDTH
    )
    mixture_heads = attention_mixture.reshape(
        count_of_rows, KEY_VALUE_HEADS, query_groups, HEAD_WIDTH
    )
    row_delta = jnp.sum(
        mixture_heads.astype(jnp.float32) * mixture_head_gradient.astype(jnp.float32), axis=3
    )
    row_delta = jnp.transpose(row_delta, (1, 2, 0))[:, :, :, None]
    dprobs = jnp.einsum(
        "tkgd,ukd->kgtu",
        mixture_head_gradient,
        value_head_split,
        preferred_element_type=jnp.float32,
    )
    dscores = (soft_weights * (dprobs - row_delta)).astype(jnp.bfloat16)
    dquery = jnp.einsum(
        "kgtu,ukd->tkgd", dscores, key_head_split, preferred_element_type=jnp.float32
    ).reshape(count_of_rows, -1) * HEAD_WIDTH ** (-0.5)
    dkeys = jnp.einsum(
        "kgtu,tkgd->ukd", dscores, query_head_split, preferred_element_type=jnp.float32
    ).reshape(key_sequence.shape[0], -1) * HEAD_WIDTH ** (-0.5)
    dvalues = jnp.einsum(
        "kgtu,tkgd->ukd", probs, mixture_head_gradient, preferred_element_type=jnp.float32
    ).reshape(key_sequence.shape[0], -1)
    return (dquery, dkeys, dvalues)


def on_device(
    inputs,
    segments,
    attn_gain,
    query_weight,
    key_weight,
    value_weight,
    output_weight,
    mlp_gain,
    gate_weight,
    up_weight,
    down_weight,
    cotangent,
):
    count_of_rows = inputs.shape[0]
    fanin = lax.axis_size("gx")
    fanout = lax.axis_size("gy")
    replicas = lax.axis_size("dp")
    begin_row = (lax.axis_index("gx") * fanout + lax.axis_index("gy")) * count_of_rows
    seq_begin = begin_row // SEQUENCE_LENGTH * SEQUENCE_LENGTH
    local_places = begin_row - seq_begin + jnp.arange(count_of_rows)
    cos_table, sin_table = rope_angles(local_places.astype(jnp.float32))
    query_segs = lax.dynamic_slice_in_dim(segments, begin_row, count_of_rows, 0)
    allowed = (jnp.arange(SEQUENCE_LENGTH)[None, :] <= local_places[:, None]) & (
        query_segs[:, None] == segments[None, :]
    )
    residual = inputs.astype(jnp.float32)
    rms_one, unit_one, normed_one = normalize(residual, attn_gain)
    q_width, k_width, v_width = (query_weight.shape[1], key_weight.shape[1], value_weight.shape[1])
    packed = jnp.concatenate([query_weight, key_weight, value_weight, output_weight], axis=1)
    attn_blocks = gather_blocks(packed)
    query_full = whole_weight(attn_blocks[:, :, :q_width])
    key_full = whole_weight(attn_blocks[:, :, q_width : q_width + k_width])
    value_full = whole_weight(attn_blocks[:, :, q_width + k_width : q_width + k_width + v_width])
    output_full = whole_weight(attn_blocks[:, :, q_width + k_width + v_width :])
    groups = fanout // fanin
    gate_part = hidden_slice(gate_weight.T, 1)
    up_part = hidden_slice(up_weight.T, 1)
    down_part = hidden_slice(down_weight, groups)
    share = gate_part.shape[0]
    gate_up_blocks = gather_blocks(jnp.concatenate([gate_part, up_part], axis=0))
    down_blocks = gather_blocks(down_part)
    model_block = gate_part.shape[1]
    gate_up_rows = (
        gate_up_blocks.reshape(fanin, fanout, 2, share, model_block)
        .transpose(2, 1, 3, 0, 4)
        .reshape(2 * fanout * share, fanin * model_block)
    )
    hidden_width = fanout * share
    down_rows = whole_weight(down_blocks)
    query_rows = jnp.dot(normed_one, query_full, preferred_element_type=jnp.float32).astype(
        jnp.bfloat16
    )
    key_rows = jnp.dot(normed_one, key_full, preferred_element_type=jnp.float32).astype(
        jnp.bfloat16
    )
    value_rows = jnp.dot(normed_one, value_full, preferred_element_type=jnp.float32).astype(
        jnp.bfloat16
    )
    rotated_query = rotate(query_rows.astype(jnp.float32), cos_table, sin_table).astype(
        jnp.bfloat16
    )
    rotated_key = rotate(key_rows.astype(jnp.float32), cos_table, sin_table).astype(jnp.bfloat16)
    kv_all = lax.all_gather(
        jnp.concatenate([rotated_key, value_rows], axis=1), ("gx", "gy"), axis=0, tiled=True
    )
    kv_width = rotated_key.shape[1]
    key_all, value_all = (kv_all[:, :kv_width], kv_all[:, kv_width:])
    attention_mixture, logsum = attend(rotated_query, key_all, value_all, allowed)
    attn_out = jnp.dot(attention_mixture, output_full, preferred_element_type=jnp.float32).astype(
        jnp.bfloat16
    )
    hidden = residual + attn_out.astype(jnp.float32)
    rms_two, unit_two, normed_two = normalize(hidden, mlp_gain)
    cot_all = lax.all_gather(cotangent, "dp", axis=0, tiled=True)
    normed_all = lax.all_gather(normed_two, "dp", axis=0, tiled=True)
    gate_up = back_product(normed_all, gate_up_rows).astype(jnp.bfloat16)
    gate_float = gate_up[:, :hidden_width].astype(jnp.float32)
    up_float = gate_up[:, hidden_width:].astype(jnp.float32)
    sigmoid_gate = jax.nn.sigmoid(gate_float)
    activated = (gate_float * sigmoid_gate * up_float).astype(jnp.bfloat16)
    dactivated = back_product(cot_all, down_rows)
    gate_delta = (
        dactivated * up_float * sigmoid_gate * (1.0 + gate_float * (1.0 - sigmoid_gate))
    ).astype(jnp.bfloat16)
    up_delta = (dactivated * gate_float * sigmoid_gate).astype(jnp.bfloat16)
    deltas = jnp.concatenate([gate_delta, up_delta], axis=1)
    dnormed_two = lax.psum_scatter(
        jnp.dot(deltas, gate_up_rows, preferred_element_type=jnp.float32).astype(jnp.bfloat16),
        "dp",
        scatter_dimension=0,
        tiled=True,
    ).astype(jnp.float32)
    mlp_out = lax.psum_scatter(
        jnp.dot(activated, down_rows, preferred_element_type=jnp.float32).astype(jnp.bfloat16),
        "dp",
        scatter_dimension=0,
        tiled=True,
    )
    layer_out = (hidden + mlp_out.astype(jnp.float32)).astype(jnp.bfloat16)
    gate_up_grad = (
        weight_product(deltas, normed_all)
        .astype(jnp.bfloat16)
        .reshape(2, fanout, share, fanin, model_block)
        .transpose(3, 1, 0, 2, 4)
        .reshape(fanin * fanout, 2 * share, model_block)
    )
    down_grad_blocks = cut_blocks(weight_product(activated, cot_all))
    if groups * share == 2 * share:
        mlp_sum = scatter_blocks(jnp.concatenate([gate_up_grad, down_grad_blocks], axis=2))
        mlp_sum = lax.all_gather(mlp_sum, "dp", axis=0, tiled=False)
        gate_up_sum, down_sum = (mlp_sum[:, :, :model_block], mlp_sum[:, :, model_block:])
    else:
        gate_up_sum = lax.all_gather(scatter_blocks(gate_up_grad), "dp", axis=0, tiled=False)
        down_sum = lax.all_gather(scatter_blocks(down_grad_blocks), "dp", axis=0, tiled=False)
    gate_grad = gate_up_sum[:, :share].reshape(replicas * share, model_block).T.astype(jnp.float32)
    up_grad = gate_up_sum[:, share:].reshape(replicas * share, model_block).T.astype(jnp.float32)
    down_grad = (
        down_sum.reshape(replicas, groups, share, -1)
        .transpose(1, 0, 2, 3)
        .reshape(down_weight.shape)
        .astype(jnp.float32)
    )
    dhidden_norm, mlpgain_part = normalize_back(dnormed_two, mlp_gain, rms_two, unit_two)
    dhidden = cotangent.astype(jnp.float32) + dhidden_norm
    dhidden_bf = dhidden.astype(jnp.bfloat16)
    output_sum = scatter_blocks(cut_blocks(weight_product(attention_mixture, dhidden_bf)))
    mixture_gradient = back_product(dhidden_bf, output_full).astype(jnp.bfloat16)
    dquery_rot, dkey_seq, dvalue_seq = attend_back(
        rotated_query, key_all, value_all, allowed, logsum, attention_mixture, mixture_gradient
    )
    dkv = lax.psum_scatter(
        jnp.concatenate([dkey_seq, dvalue_seq], axis=1).astype(jnp.bfloat16),
        ("gx", "gy"),
        scatter_dimension=0,
        tiled=True,
    )
    dquery = unrotate(dquery_rot, cos_table, sin_table).astype(jnp.bfloat16)
    query_sum = scatter_blocks(cut_blocks(weight_product(normed_one, dquery)))
    dkey = unrotate(dkv[:, :kv_width].astype(jnp.float32), cos_table, sin_table).astype(
        jnp.bfloat16
    )
    dvalue_bf = dkv[:, kv_width:]
    kv_sum = scatter_blocks(
        jnp.concatenate(
            [
                cut_blocks(weight_product(normed_one, dkey)),
                cut_blocks(weight_product(normed_one, dvalue_bf)),
            ],
            axis=2,
        )
    )
    dnormed_one = (
        back_product(dquery, query_full)
        + back_product(dkey, key_full)
        + back_product(dvalue_bf, value_full)
    )
    dresidual, attgain_part = normalize_back(dnormed_one, attn_gain, rms_one, unit_one)
    input_grad = (dhidden + dresidual).astype(jnp.bfloat16)
    gain_parts = lax.all_gather(
        jnp.stack([attgain_part, mlpgain_part]), ("dp", "gx", "gy"), axis=0, tiled=False
    )
    attgain_grad, mlpgain_grad = jnp.sum(gain_parts, axis=0)
    attn_sum = lax.psum(jnp.concatenate([output_sum, query_sum, kv_sum], axis=1), "dp").astype(
        jnp.float32
    )
    o_width = output_weight.shape[1]
    output_grad = attn_sum[:, :o_width]
    query_grad = attn_sum[:, o_width : o_width + q_width]
    key_grad = attn_sum[:, o_width + q_width : o_width + q_width + k_width]
    value_grad = attn_sum[:, o_width + q_width + k_width :]
    return (
        layer_out,
        input_grad,
        query_grad,
        key_grad,
        value_grad,
        output_grad,
        gate_grad,
        up_grad,
        down_grad,
        attgain_grad,
        mlpgain_grad,
    )


def solution(mesh):
    return jax.shard_map(
        on_device,
        mesh=mesh,
        in_specs=(
            P(("dp", "gx", "gy"), None),
            P("dp"),
            P(),
            P("gx", "gy"),
            P("gx", "gy"),
            P("gx", "gy"),
            P("gx", "gy"),
            P(),
            P("gx", "gy"),
            P("gx", "gy"),
            P("gx", "gy"),
            P(("dp", "gx", "gy"), None),
        ),
        out_specs=(
            P(("dp", "gx", "gy"), None),
            P(("dp", "gx", "gy"), None),
            P("gx", "gy"),
            P("gx", "gy"),
            P("gx", "gy"),
            P("gx", "gy"),
            P("gx", "gy"),
            P("gx", "gy"),
            P("gx", "gy"),
            P(),
            P(),
        ),
        check_vma=False,
    )
```

profile of v0, /device:TPU:0, one launch (start us, length us, event | category | flops | bytes accessed | tf_op | source)
XLA Modules:
  0.0 793.3 jit_solution(703122421121879821)
XLA Ops:
  14.5 81.8 %all-gather.16.cloned.1.call-done = bf16[3840,640]{1,0:T(8,128)(2,1)} async-done(((bf16[480,640]{1,0:T(8,128)(2,1)}), bf16[3840,640]{1,0:T(8,128)(2,1)}) %all-gather.16.cloned.1.call-update) | async-done | bytes 4915216 | tf_op jit(solution)/shard_map/all_gather | solution.py:79
  96.3 2.8 fusion.62
  104.5 10.1 %all_gather.40 = bf16[512,960]{0,1:T(8,128)(2,1)} all-gather(bf16[128,960]{0,1:T(8,128)(2,1)S(1)} %copy-done.18), channel_id=1, replica_groups=mesh['dp'=4,'gx'=2,'gy'=4] {'dp'}, dimensions={0}, use_global_device_ids=true | all-gather | bytes 1228800 | tf_op jit(solution)/shard_map/all_gather | solution.py:260
  114.6 24.4 %all-gather.12.cloned.1.call-done = bf16[8,320,240]{2,1,0:T(8,128)(2,1)} async-done(((bf16[1,320,240]{2,1,0:T(8,128)(2,1)}), bf16[8,320,240]{2,1,0:T(8,128)(2,1)}) %all-gather.12.cloned.1.call-update) | async-done | bytes 1228816 | tf_op jit(solution)/shard_map/all_gather | solution.py:79
  139.0 2.3 copy.179
  143.4 51.5 %all-gather.18.cloned.1.call-done = bf16[2560,480]{1,0:T(8,128)(2,1)} async-done(((bf16[320,480]{1,0:T(8,128)(2,1)}), bf16[2560,480]{1,0:T(8,128)(2,1)}) %all-gather.18.cloned.1.call-update) | async-done | bytes 2457616 | tf_op jit(solution)/shard_map/all_gather | solution.py:79
  194.9 5.9 copy.137
  200.8 5.7 reshape.309
  206.6 4.5 fusion.61
  211.0 2.8 copy.132
  213.8 3.9 reshape.299
  219.3 2.9 copy.134
  222.2 5.0 reshape.303
  227.3 10.2 %all-gather.10.cloned.1.call-done = bf16[1024,640]{0,1:T(8,128)(2,1)} async-done(((bf16[128,640]{0,1:T(8,128)(2,1)}), bf16[1024,640]{0,1:T(8,128)(2,1)}) %all-gather.10.cloned.1.call-update) | async-done | bytes 1310736 | tf_op jit(solution)/shard_map/all_gather | solution.py:249
  246.6 9.7 %all_gather.36 = bf16[512,960]{0,1:T(8,128)(2,1)S(1)} all-gather(bf16[128,960]{0,1:T(8,128)(2,1)S(1)} %multiply_convert_fusion), channel_id=1, replica_groups=mesh['dp'=4,'gx'=2,'gy'=4] {'dp'}, dimensions={0}, use_global_device_ids=true | all-gather | bytes 1228800 | tf_op jit(solution)/shard_map/all_gather | solution.py:261
  260.7 2.4 convolution_convert_fusion.5
  265.9 3.7 convolution_convert_fusion.6
  269.6 2.3 copy.170
  272.0 16.0 %reduce-scatter.24.cloned.1.call-done = bf16[128,960]{1,0:T(8,128)(2,1)} async-done(((bf16[512,960]{1,0:T(8,128)(2,1)}), bf16[128,960]{1,0:T(8,128)(2,1)}) %reduce-scatter.24.cloned.1.call-update) | async-done | bytes 245776
  289.5 26.3 %reduce-scatter.22.cloned.1.call-done = bf16[128,960]{1,0:T(8,128)(2,1)} async-done(((bf16[512,960]{1,0:T(8,128)(2,1)}), bf16[128,960]{1,0:T(8,128)(2,1)}) %reduce-scatter.22.cloned.1.call-update) | async-done | bytes 245776
  317.5 2.3 fusion.29
  322.2 5.4 fusion.6
  327.6 2.8 fusion.1
  333.4 2.5 copy.174
  338.0 6.0 reshape.317
  344.0 3.2 copy.144
  347.4 3.1 convolution_multiply_fusion
  352.7 6.1 reshape.319
  358.7 3.1 copy.145
  361.9 39.3 %reduce-scatter.26.cloned.1.call-done = bf16[128,640]{1,0:T(8,128)(2,1)} async-done(((bf16[1024,640]{1,0:T(8,128)(2,1)}), bf16[128,640]{1,0:T(8,128)(2,1)}) %reduce-scatter.26.cloned.1.call-update) | async-done | bytes 163856
  403.6 3.5 reshape.321
  407.1 3.5 copy.146
  412.1 3.5 reshape.323
  415.6 3.6 copy.147
  419.1 3.7 pad_maximum_fusion.1
  423.1 4.5 convolution_convert_fusion
  427.6 4.4 copy.148
  432.0 5.8 reshape.325
  437.9 3.9 copy.149
  443.8 4.4 reshape.350
  448.2 5.1 copy.169
  455.5 3.1 pad_maximum_fusion
  458.6 12.5 %reduce-scatter.14.cloned.1.call-done = bf16[1,480,240]{2,1,0:T(8,128)(2,1)} async-done(((bf16[8,480,240]{2,1,0:T(8,128)(2,1)}), bf16[1,480,240]{2,1,0:T(8,128)(2,1)}) %reduce-scatter.14.cloned.1.call-update) | async-done | bytes 230416 | tf_op jit(solution)/shard_map/reduce_scatter | solution.py:99
  471.1 69.8 %reduce-scatter.16.cloned.1.call-done = bf16[1,480,240]{2,1,0:T(8,128)(2,1)} async-done(((bf16[8,480,240]{2,1,0:T(8,128)(2,1)}), bf16[1,480,240]{2,1,0:T(8,128)(2,1)}) %reduce-scatter.16.cloned.1.call-update) | async-done | bytes 230416 | tf_op jit(solution)/shard_map/reduce_scatter | solution.py:99
  540.9 69.8 %reduce-scatter.18.cloned.1.call-done = bf16[1,480,160]{2,1,0:T(8,128)(2,1)} async-done(((bf16[8,480,160]{2,1,0:T(8,128)(2,1)}), bf16[1,480,160]{2,1,0:T(8,128)(2,1)}) %reduce-scatter.18.cloned.1.call-update) | async-done | bytes 153616 | tf_op jit(solution)/shard_map/reduce_scatter | solution.py:99
  610.7 2.3 pad_maximum_fusion.7
  613.1 85.0 %reduce-scatter.20.cloned.1.call-done = bf16[1,320,720]{2,1,0:T(8,128)(2,1)} async-done(((bf16[8,320,720]{2,1,0:T(8,128)(2,1)}), bf16[1,320,720]{2,1,0:T(8,128)(2,1)}) %reduce-scatter.20.cloned.1.call-update) | async-done | bytes 460816 | tf_op jit(solution)/shard_map/reduce_scatter | solution.py:99
  702.7 69.5 %all-gather.3 = f32[32,2,960]{2,1,0:T(2,128)S(1)} all-gather(f32[1,2,960]{2,1,0:T(2,128)S(1)} %maximum_bitcast_fusion), channel_id=4, replica_groups=mesh['dp'=4,'gx'=2,'gy'=4] {'dp','gx','gy'}, dimensions={0}, use_global_device_ids=true | all-gather | bytes 253440 | tf_op jit(solution)/shard_map/all_gather | solution.py:345
  (188 shorter events, 72.6 us)
Async XLA Ops:
  7.2 4.5 copy-start.24
  7.2 89.1 %all-gather.16.cloned.1.call-start = ((), (), s32[]{:S(2)}) async-start(), calls=%async_computation.15 | async-start | bytes 5529600 | tf_op jit(solution)/shard_map/all_gather | solution.py:79
  8.3 4.4 copy-start.25
  11.6 1.4 copy-start.26
  11.7 127.3 %all-gather.12.cloned.1.call-start = ((), (), s32[]{:S(2)}) async-start(), calls=%async_computation.8 | async-start | bytes 1474560 | tf_op jit(solution)/shard_map/all_gather | solution.py:79
  12.7 1.5 copy-start.3
  12.7 182.2 %all-gather.18.cloned.1.call-start = ((), (), s32[]{:S(2)}) async-start(), calls=%async_computation.16 | async-start | bytes 2949120 | tf_op jit(solution)/shard_map/all_gather | solution.py:79
  14.1 223.4 %all-gather.10.cloned.1.call-start = ((), (), s32[]{:S(2)}) async-start(), calls=%async_computation.7 | async-start | bytes 1474560 | tf_op jit(solution)/shard_map/all_gather | solution.py:249
  99.2 1.4 copy-start.28
  102.2 1.9 copy-start.30
  102.2 2.2 copy-start.18
  102.9 36.1 %copy-start.10 = (bf16[960,320]{0,1:T(8,128)(2,1)}, bf16[960,320]{0,1:T(8,128)(2,1)S(1)}, u32[]{:S(2)}) copy-start(bf16[960,320]{0,1:T(8,128)(2,1)S(1)} %reshape.295) | copy-start | bytes 1843204
  104.1 183.9 %reduce-scatter.24.cloned.1.call-start = ((), (), s32[]{:S(2)}) async-start(), calls=%async_computation.18 | async-start | bytes 1310720
  104.4 137.5 %copy-start.16 = (pred[128,1024]{0,1:T(8,128)(4,1)}, pred[128,1024]{0,1:T(8,128)(4,1)S(1)}, u32[]{:S(2)}) copy-start(pred[128,1024]{0,1:T(8,128)(4,1)S(1)} %fusion.26) | copy-start | bytes 393220
  217.7 1.5 copy-start.5
  238.9 1.4 copy-start.6
  238.9 3.0 copy-start.22
  240.3 3.1 copy-start
  243.4 2.0 copy-start.2
  245.4 10.8 %copy-start.12 = (bf16[5,64,3,128]{3,1,2,0:T(8,128)(2,1)}, bf16[5,64,3,128]{3,1,2,0:T(8,128)(2,1)S(1)}, u32[]{:S(2)}) copy-start(bf16[5,64,3,128]{3,1,2,0:T(8,128)(2,1)S(1)} %convolution_convert_fusion.12) | copy-start | bytes 737284
  245.4 1.0 copy-start.29
  245.4 10.8 %copy-start.8 = (bf16[1280,960]{1,0:T(8,128)(2,1)S(1)}, bf16[1280,960]{1,0:T(8,128)(2,1)}, u32[]{:S(2)}) copy-start(bf16[1280,960]{1,0:T(8,128)(2,1)} %reshape.309) | copy-start | bytes 7372804
  256.2 1.6 copy-start.21
  256.2 1.7 copy-start.15
  256.2 1.9 copy-start.19
  258.2 1.4 copy-start.33
  259.6 1.1 copy-start.32
  265.5 50.3 %reduce-scatter.22.cloned.1.call-start = ((), (), s32[]{:S(2)}) async-start(), calls=%async_computation.17 | async-start | bytes 1310720
  271.9 129.3 %reduce-scatter.26.cloned.1.call-start = ((), (), s32[]{:S(2)}) async-start(), calls=%async_computation.19 | async-start | bytes 1474560
  289.1 26.6 %copy-start.11 = (bf16[128,960]{0,1:T(8,128)(2,1)}, bf16[128,960]{0,1:T(8,128)(2,1)S(1)}, u32[]{:S(2)}) copy-start(bf16[128,960]{0,1:T(8,128)(2,1)S(1)} %copy.173) | copy-start | bytes 737284
  317.5 4.5 copy-start.13
  317.5 10.0 %slice-start = ((s8[7864320]{0:T(1024)(128)(4,1)}), s8[4194304]{0:T(1024)(128)(4,1)S(1)}, s32[]{:S(2)}) async-start(s8[7864320]{0:T(1024)(128)(4,1)} %bitcast.180), calls=%async_computation.20 | async-start | bytes 8388608
  319.8 2.4 copy-start.17
  322.2 5.4 slice-start.1
  322.2 5.4 copy-start.23
  330.4 1.9 copy-start.1
  333.4 2.5 copy-start.14
  335.9 135.2 %reduce-scatter.14.cloned.1.call-start = ((), (), s32[]{:S(2)}) async-start(), calls=%async_computation.9 | async-start | bytes 2211840 | tf_op jit(solution)/shard_map/reduce_scatter | solution.py:99
  347.2 193.7 %reduce-scatter.16.cloned.1.call-start = ((), (), s32[]{:S(2)}) async-start(), calls=%async_computation.10 | async-start | bytes 2211840 | tf_op jit(solution)/shard_map/reduce_scatter | solution.py:99
  361.9 248.8 %reduce-scatter.18.cloned.1.call-start = ((), (), s32[]{:S(2)}) async-start(), calls=%async_computation.11 | async-start | bytes 2211840 | tf_op jit(solution)/shard_map/reduce_scatter | solution.py:99
  402.3 8.3 %copy-start.27 = (bf16[128,640]{1,0:T(8,128)(2,1)S(1)}, bf16[128,640]{1,0:T(8,128)(2,1)}, u32[]{:S(2)}) copy-start(bf16[128,640]{1,0:T(8,128)(2,1)} %reduce-scatter.26.cloned.1.call-done) | copy-start | bytes 491524
  422.8 275.2 %reduce-scatter.20.cloned.1.call-start = ((), (), s32[]{:S(2)}) async-start(), calls=%async_computation.13 | async-start | bytes 4423680 | tf_op jit(solution)/shard_map/reduce_scatter | solution.py:99
  437.8 3.9 copy-start.20
  437.9 3.9 copy-start.34
  453.3 2.1 copy-start.4
  458.6 316.3 %all-reduce.2.cloned.1.call-start = ((), (), s32[]{:S(2)}) async-start(), calls=%async_computation.12 | async-start | bytes 1228800 | tf_op jit(solution)/shard_map/psum | solution.py:349
  613.0 165.7 %all-gather.14.cloned.1.call-start = ((), (), s32[]{:S(2)}) async-start(), calls=%async_computation.14 | async-start | bytes 2457600 | tf_op jit(solution)/shard_map/all_gather | solution.py:296
  774.9 2.8 copy-start.7
  (2 other events, 1.7 us)
Sparse Core Ops, SparseCore 0:
  11.8 84.5 all-gather.15
  99.0 39.9 all-gather.11
  141.6 53.2 all-gather.17
  197.3 40.1 all-gather.9
  265.6 22.3 reduce-scatter.23
  290.9 24.7 reduce-scatter.21
  336.1 65.1 reduce-scatter.25
  404.7 66.4 reduce-scatter.13
  474.6 66.2 reduce-scatter.15
  544.2 66.4 reduce-scatter.17
  614.4 83.6 reduce-scatter.19
  700.9 33.4 all-reduce.1
  735.9 22.0 all-gather.13
where the time goes:
time: 800 us; the launch traced here: 793 us
  waiting for transfers between devices  487 us (61%)
  local copies, waits for them, and re-layouts  131 us (16%)
  blocking collectives  89.3 us (11%)
  matrix products  48.1 us (6%)
  other arithmetic  21.8 us (3%)
  between operations  14.9 us (2%)
    reduce_scatter x4, waiting for transfers between devices, scatter_blocks(): lax.psum_scatter(blocks, ('gx', 'gy'), scatter_dimension=0, tiled=False)  237 us
    all_gather x3, waiting for transfers between devices, gather_blocks(): return lax.all_gather(block, ('gx', 'gy'), axis=0, tiled=False)  158 us
    unnamed x16, waiting for transfers between devices  81.7 us
    all_gather x1, blocking collectives, on_device(): lax.all_gather(jnp.stack([attgain_part, mlpgain_part]), ('dp', 'gx', 'gy'...  69.5 us
    reshape x6, local copies, waits for them, and re-layouts, cut_blocks(): grad.astype(jnp.bfloat16).reshape(fanin, rows, fanout, columns)  28.6 us
    unnamed x90, local copies, waits for them, and re-layouts  23.7 us
  transfers between devices with their start and end apart: 13, of which 11 were waited for; matrix products, arithmetic and copies ran while one was open for 19% of the time, Pallas kernels for 0%

commit v1 on v0

--- a/solution.py
+++ b/solution.py
@@ -257,8 +257,11 @@
     )
     hidden = residual + attn_out.astype(jnp.float32)
     rms_two, unit_two, normed_two = normalize(hidden, mlp_gain)
-    cot_all = lax.all_gather(cotangent, "dp", axis=0, tiled=True)
-    normed_all = lax.all_gather(normed_two, "dp", axis=0, tiled=True)
+    cot_all, normed_all = jnp.split(
+        lax.all_gather(jnp.concatenate([cotangent, normed_two], axis=1), "dp", axis=0, tiled=True),
+        [cotangent.shape[1]],
+        axis=1,
+    )
     gate_up = back_product(normed_all, gate_up_rows).astype(jnp.bfloat16)
     gate_float = gate_up[:, :hidden_width].astype(jnp.float32)
     up_float = gate_up[:, hidden_width:].astype(jnp.float32)

time: 800 us -> 815 us (1.019)
  waiting for transfers between devices: 487 us -> 513 us
  blocking collectives: 89.3 us -> 69.5 us
    all_gather x2 -> x0, blocking collectives: 19.8 us -> none  [the longest x1 10.1 us: on_device(): cot_all = lax.all_gather(cotangent, 'dp', axis=0, tiled=True)]
    all_gather x0 -> x1, waiting for transfers between devices: none -> 10.8 us  [on_device(): lax.all_gather(jnp.concatenate([cotangent, normed_two], axis=1), 'dp', ax...]
    unnamed x16 -> x17, waiting for transfers between devices: 81.7 us -> 84.2 us
    unnamed x90 -> x86, local copies, waits for them, and re-layouts: 23.7 us -> 24.3 us
  transfers between devices with their start and end apart: 13 -> 14, of which waited for: 11 -> 12; matrix products, arithmetic and copies ran while one was open for 19% -> 19% of each run, Pallas kernels for 0% -> 0%
where the time goes in v1:
time: 815 us; the launch traced here: 807 us
  waiting for transfers between devices  513 us (63%)
  local copies, waits for them, and re-layouts  135 us (17%)
  blocking collectives  69.5 us (9%)
  matrix products  50.4 us (6%)
  other arithmetic  22.4 us (3%)
  between operations  14.9 us (2%)
    reduce_scatter x4, waiting for transfers between devices, scatter_blocks(): lax.psum_scatter(blocks, ('gx', 'gy'), scatter_dimension=0, tiled=False)  237 us
    all_gather x3, waiting for transfers between devices, gather_blocks(): return lax.all_gather(block, ('gx', 'gy'), axis=0, tiled=False)  166 us
    unnamed x17, waiting for transfers between devices  84.2 us
    all_gather x1, blocking collectives, on_device(): lax.all_gather(jnp.stack([attgain_part, mlpgain_part]), ('dp', 'gx', 'gy'...  69.5 us
    reshape x6, local copies, waits for them, and re-layouts, cut_blocks(): grad.astype(jnp.bfloat16).reshape(fanin, rows, fanout, columns)  28.6 us
    unnamed x86, local copies, waits for them, and re-layouts  24.3 us
  transfers between devices with their start and end apart: 14, of which 12 were waited for; matrix products, arithmetic and copies ran while one was open for 19% of the time, Pallas kernels for 0%

profile of v1, /device:TPU:0, one launch (start us, length us, event | category | flops | bytes accessed | tf_op | source)
XLA Modules:
  0.0 806.9 jit_solution(106580712702877046)
XLA Ops:
  12.0 84.3 %all-gather.19.cloned.1.call-done = bf16[3840,640]{1,0:T(8,128)(2,1)} async-done(((bf16[480,640]{1,0:T(8,128)(2,1)}), bf16[3840,640]{1,0:T(8,128)(2,1)}) %all-gather.19.cloned.1.call-update) | async-done | bytes 4915216 | tf_op jit(solution)/shard_map/all_gather | solution.py:79
  96.3 2.8 fusion.67
  107.9 4.6 fusion.66
  112.4 2.8 copy.128
  115.3 4.1 reshape.299
  120.9 2.8 copy.130
  123.7 4.8 reshape.303
  128.7 15.3 %all-gather.11.cloned.1.call-done = bf16[1024,640]{0,1:T(8,128)(2,1)} async-done(((bf16[128,640]{0,1:T(8,128)(2,1)}), bf16[1024,640]{0,1:T(8,128)(2,1)}) %all-gather.11.cloned.1.call-update) | async-done | bytes 1310736 | tf_op jit(solution)/shard_map/all_gather | solution.py:249
  154.1 32.8 %all-gather.15.cloned.1.call-done = bf16[8,320,240]{2,1,0:T(8,128)(2,1)} async-done(((bf16[1,320,240]{2,1,0:T(8,128)(2,1)}), bf16[8,320,240]{2,1,0:T(8,128)(2,1)}) %all-gather.15.cloned.1.call-update) | async-done | bytes 1228816 | tf_op jit(solution)/shard_map/all_gather | solution.py:79
  186.9 3.4 copy.173
  190.2 3.9 reshape.312
  194.2 48.5 %all-gather.21.cloned.1.call-done = bf16[2560,480]{1,0:T(8,128)(2,1)} async-done(((bf16[320,480]{1,0:T(8,128)(2,1)}), bf16[2560,480]{1,0:T(8,128)(2,1)}) %all-gather.21.cloned.1.call-update) | async-done | bytes 2457616 | tf_op jit(solution)/shard_map/all_gather | solution.py:79
  242.7 6.1 copy.133
  248.7 5.8 reshape.309
  254.5 10.8 %all-gather.13.cloned.1.call-done = bf16[512,1920]{0,1:T(8,128)(2,1)} async-done(((bf16[128,1920]{0,1:T(8,128)(2,1)}), bf16[512,1920]{0,1:T(8,128)(2,1)}) %all-gather.13.cloned.1.call-update) | async-done | bytes 1966096 | tf_op jit(solution)/shard_map/all_gather | solution.py:261
  265.3 3.8 convolution_convert_fusion.1
  271.6 2.4 convolution_convert_fusion.5
  276.4 3.7 convolution_convert_fusion.6
  282.9 18.4 %reduce-scatter.24.cloned.1.call-done = bf16[128,960]{1,0:T(8,128)(2,1)} async-done(((bf16[512,960]{1,0:T(8,128)(2,1)}), bf16[128,960]{1,0:T(8,128)(2,1)}) %reduce-scatter.24.cloned.1.call-update) | async-done | bytes 245776
  302.8 26.4 %reduce-scatter.22.cloned.1.call-done = bf16[128,960]{1,0:T(8,128)(2,1)} async-done(((bf16[512,960]{1,0:T(8,128)(2,1)}), bf16[128,960]{1,0:T(8,128)(2,1)}) %reduce-scatter.22.cloned.1.call-update) | async-done | bytes 245776
  331.0 2.3 fusion.34
  335.7 5.4 fusion.6
  341.1 2.8 fusion.1
  346.9 2.5 copy.168
  351.5 6.0 reshape.317
  357.5 3.1 copy.139
  360.6 3.1 convolution_multiply_fusion
  365.9 6.0 reshape.319
  372.0 3.2 copy.140
  375.4 39.2 %reduce-scatter.26.cloned.1.call-done = bf16[128,640]{1,0:T(8,128)(2,1)} async-done(((bf16[1024,640]{1,0:T(8,128)(2,1)}), bf16[128,640]{1,0:T(8,128)(2,1)}) %reduce-scatter.26.cloned.1.call-update) | async-done | bytes 163856
  417.0 3.5 reshape.321
  420.5 3.5 copy.141
  425.4 3.5 reshape.323
  428.9 3.6 copy.142
  432.5 3.6 pad_maximum_fusion.1
  436.2 4.6 convolution_convert_fusion
  440.7 4.5 copy.143
  445.3 5.8 reshape.325
  451.1 3.9 copy.144
  457.1 4.4 reshape.350
  461.5 5.2 copy.163
  468.8 3.0 pad_maximum_fusion
  471.8 12.7 %reduce-scatter.14.cloned.1.call-done = bf16[1,480,240]{2,1,0:T(8,128)(2,1)} async-done(((bf16[8,480,240]{2,1,0:T(8,128)(2,1)}), bf16[1,480,240]{2,1,0:T(8,128)(2,1)}) %reduce-scatter.14.cloned.1.call-update) | async-done | bytes 230416 | tf_op jit(solution)/shard_map/reduce_scatter | solution.py:99
  484.6 70.0 %reduce-scatter.16.cloned.1.call-done = bf16[1,480,240]{2,1,0:T(8,128)(2,1)} async-done(((bf16[8,480,240]{2,1,0:T(8,128)(2,1)}), bf16[1,480,240]{2,1,0:T(8,128)(2,1)}) %reduce-scatter.16.cloned.1.call-update) | async-done | bytes 230416 | tf_op jit(solution)/shard_map/reduce_scatter | solution.py:99
  554.5 70.1 %reduce-scatter.18.cloned.1.call-done = bf16[1,480,160]{2,1,0:T(8,128)(2,1)} async-done(((bf16[8,480,160]{2,1,0:T(8,128)(2,1)}), bf16[1,480,160]{2,1,0:T(8,128)(2,1)}) %reduce-scatter.18.cloned.1.call-update) | async-done | bytes 153616 | tf_op jit(solution)/shard_map/reduce_scatter | solution.py:99
  624.7 2.3 pad_maximum_fusion.7
  627.2 84.5 %reduce-scatter.20.cloned.1.call-done = bf16[1,320,720]{2,1,0:T(8,128)(2,1)} async-done(((bf16[8,320,720]{2,1,0:T(8,128)(2,1)}), bf16[1,320,720]{2,1,0:T(8,128)(2,1)}) %reduce-scatter.20.cloned.1.call-update) | async-done | bytes 460816 | tf_op jit(solution)/shard_map/reduce_scatter | solution.py:99
  716.4 69.5 %all-gather.3 = f32[32,2,960]{2,1,0:T(2,128)S(1)} all-gather(f32[1,2,960]{2,1,0:T(2,128)S(1)} %maximum_bitcast_fusion), channel_id=4, replica_groups=mesh['dp'=4,'gx'=2,'gy'=4] {'dp','gx','gy'}, dimensions={0}, use_global_device_ids=true | all-gather | bytes 253440 | tf_op jit(solution)/shard_map/all_gather | solution.py:348
  (186 shorter events, 72.9 us)
Async XLA Ops:
  7.2 4.5 copy-start.3
  7.2 89.1 %all-gather.19.cloned.1.call-start = ((), (), s32[]{:S(2)}) async-start(), calls=%async_computation.16 | async-start | bytes 5529600 | tf_op jit(solution)/shard_map/all_gather | solution.py:79
  11.6 132.4 %all-gather.11.cloned.1.call-start = ((), (), s32[]{:S(2)}) async-start(), calls=%async_computation.7 | async-start | bytes 1474560 | tf_op jit(solution)/shard_map/all_gather | solution.py:249
  99.1 1.4 copy-start.24
  100.5 0.8 copy-start.9
  102.1 1.9 copy-start.21
  102.8 2.6 copy-start.10
  102.8 2.3 copy-start.22
  104.0 82.9 %all-gather.15.cloned.1.call-start = ((), (), s32[]{:S(2)}) async-start(), calls=%async_computation.9 | async-start | bytes 1474560 | tf_op jit(solution)/shard_map/all_gather | solution.py:79
  105.0 2.6 copy-start.26
  105.0 137.6 %all-gather.21.cloned.1.call-start = ((), (), s32[]{:S(2)}) async-start(), calls=%async_computation.17 | async-start | bytes 2949120 | tf_op jit(solution)/shard_map/all_gather | solution.py:79
  107.5 157.8 %all-gather.13.cloned.1.call-start = ((), (), s32[]{:S(2)}) async-start(), calls=%async_computation.8 | async-start | bytes 2457600 | tf_op jit(solution)/shard_map/all_gather | solution.py:261
  107.9 40.5 %copy-start.16 = (pred[128,1024]{0,1:T(8,128)(4,1)}, pred[128,1024]{0,1:T(8,128)(4,1)S(1)}, u32[]{:S(2)}) copy-start(pred[128,1024]{0,1:T(8,128)(4,1)S(1)} %fusion.31) | copy-start | bytes 393220
  119.3 1.6 copy-start.5
  145.4 1.4 copy-start.6
  145.4 3.0 copy-start.19
  146.8 3.1 copy-start
  149.8 2.0 copy-start.2
  151.8 2.0 copy-start.12
  151.8 1.0 copy-start.25
  151.8 1.2 copy-start.18
  153.8 147.5 %reduce-scatter.24.cloned.1.call-start = ((), (), s32[]{:S(2)}) async-start(), calls=%async_computation.19 | async-start | bytes 1310720
  265.3 3.8 copy-start.15
  265.3 3.8 copy-start.27
  269.1 1.4 copy-start.31
  269.1 2.5 copy-start.8
  270.5 1.1 copy-start.30
  276.3 52.9 %reduce-scatter.22.cloned.1.call-start = ((), (), s32[]{:S(2)}) async-start(), calls=%async_computation.18 | async-start | bytes 1310720
  282.4 132.2 %reduce-scatter.26.cloned.1.call-start = ((), (), s32[]{:S(2)}) async-start(), calls=%async_computation.20 | async-start | bytes 1474560
  302.4 26.8 %copy-start.11 = (bf16[128,960]{0,1:T(8,128)(2,1)}, bf16[128,960]{0,1:T(8,128)(2,1)S(1)}, u32[]{:S(2)}) copy-start(bf16[128,960]{0,1:T(8,128)(2,1)S(1)} %copy.167) | copy-start | bytes 737284
  331.0 4.5 copy-start.13
  331.0 10.0 %slice-start = ((s8[7864320]{0:T(1024)(128)(4,1)}), s8[4194304]{0:T(1024)(128)(4,1)S(1)}, s32[]{:S(2)}) async-start(s8[7864320]{0:T(1024)(128)(4,1)} %bitcast.174), calls=%async_computation.21 | async-start | bytes 8388608
  333.3 2.4 copy-start.17
  335.6 5.4 slice-start.1
  335.6 5.4 copy-start.20
  343.8 1.9 copy-start.1
  346.9 2.6 copy-start.14
  349.4 135.2 %reduce-scatter.14.cloned.1.call-start = ((), (), s32[]{:S(2)}) async-start(), calls=%async_computation.10 | async-start | bytes 2211840 | tf_op jit(solution)/shard_map/reduce_scatter | solution.py:99
  360.6 193.9 %reduce-scatter.16.cloned.1.call-start = ((), (), s32[]{:S(2)}) async-start(), calls=%async_computation.11 | async-start | bytes 2211840 | tf_op jit(solution)/shard_map/reduce_scatter | solution.py:99
  375.2 249.5 %reduce-scatter.18.cloned.1.call-start = ((), (), s32[]{:S(2)}) async-start(), calls=%async_computation.12 | async-start | bytes 2211840 | tf_op jit(solution)/shard_map/reduce_scatter | solution.py:99
  415.7 8.3 %copy-start.23 = (bf16[128,640]{1,0:T(8,128)(2,1)S(1)}, bf16[128,640]{1,0:T(8,128)(2,1)}, u32[]{:S(2)}) copy-start(bf16[128,640]{1,0:T(8,128)(2,1)} %reduce-scatter.26.cloned.1.call-done) | copy-start | bytes 491524
  436.1 275.6 %reduce-scatter.20.cloned.1.call-start = ((), (), s32[]{:S(2)}) async-start(), calls=%async_computation.14 | async-start | bytes 4423680 | tf_op jit(solution)/shard_map/reduce_scatter | solution.py:99
  451.1 3.9 copy-start.28
  451.1 3.9 copy-start.32
  466.7 2.1 copy-start.4
  471.8 316.7 %all-reduce.2.cloned.1.call-start = ((), (), s32[]{:S(2)}) async-start(), calls=%async_computation.13 | async-start | bytes 1228800 | tf_op jit(solution)/shard_map/psum | solution.py:352
  627.0 165.4 %all-gather.17.cloned.1.call-start = ((), (), s32[]{:S(2)}) async-start(), calls=%async_computation.15 | async-start | bytes 2457600 | tf_op jit(solution)/shard_map/all_gather | solution.py:299
  788.5 2.8 copy-start.7
  (1 other events, 0.8 us)
Sparse Core Ops, SparseCore 0:
  11.7 84.5 all-gather.18
  104.1 39.8 all-gather.10
  146.7 40.1 all-gather.14
  189.4 53.2 all-gather.20
  244.6 20.6 all-gather.12
  276.5 24.7 reduce-scatter.23
  304.4 24.7 reduce-scatter.21
  349.5 65.0 reduce-scatter.25
  418.1 66.4 reduce-scatter.13
  487.9 66.6 reduce-scatter.15
  558.0 66.6 reduce-scatter.17
  628.2 83.5 reduce-scatter.19
  714.7 33.4 all-reduce.1
  749.7 21.9 all-gather.16
